TPU v7x, 32 devices: a whole 2x2x4 slice. The times are simulated.
32 devices in a mesh: dp: 4 (over y, x), depth: 4 (over z), grid: 2 (over core).
Axes of the slice: x: 2, y: 2, z: 4, core: 2. Of those that a mesh axis runs over, the one named last changes fastest.
Arguments:
- tokens: bfloat16 [1024, 12288], P(('dp', 'depth'), 'grid'), may hold values from -6 to 6
- weight: bfloat16 [12288, 24576], P('grid', 'depth'), may hold values from -0.0546875 to 0.0546875
- cotangent: bfloat16 [1024, 24576], P(('dp', 'grid'), 'depth'), may hold values from -0.5 to 0.5
Outputs:
- hidden: bfloat16 [1024, 24576], P(('dp', 'grid'), 'depth')
- weight_grad: bfloat16 [12288, 24576], P(('grid', 'dp'), 'depth')
All inputs are finite; a program needn't handle non-finite values.
Results may differ from a plain program's by a relative error of at most 0.011.
Values may be sent and summed in bfloat16 or wider, within the bound.
No kernel may reach another device: no remote copies, remote signals or barrier semaphores. Data moves between devices by JAX's collectives and lax.ppermute only.
A program may use at most 192 MiB of HBM per device.

v0:
```python
import jax
import jax.numpy as jnp
from jax import lax
from jax.sharding import PartitionSpec as P


def gelu_tanh(values):
    return jax.nn.gelu(values, approximate=True)


def transposed_product(left, right):
    return lax.dot_general(
        left, right, (((0,), (0,)), ((), ())), preferred_element_type=jnp.float32
    )


def local(tokens, weight, cotangent):
    all_rows = lax.all_gather(tokens, ("dp", "depth"), axis=0, tiled=True)
    group_size = all_rows.shape[0] // lax.axis_size("dp")
    own_rows = lax.dynamic_slice_in_dim(all_rows, lax.axis_index("dp") * group_size, group_size, 0)
    partial_pre = jnp.dot(own_rows, weight, preferred_element_type=jnp.float32)
    preact = lax.psum_scatter(partial_pre, "grid", scatter_dimension=0, tiled=True)
    activated, pullback = jax.vjp(gelu_tanh, preact)
    hidden = activated.astype(jnp.bfloat16)
    grad_pre = pullback(cotangent.astype(jnp.float32))[0].astype(jnp.bfloat16)
    sub_width = all_rows.shape[1] // lax.axis_size("dp")
    columns = lax.dynamic_slice_in_dim(all_rows, lax.axis_index("dp") * sub_width, sub_width, 1)
    weight_grad = transposed_product(
        columns, lax.all_gather(grad_pre, ("dp", "grid"), axis=0, tiled=True)
    )
    return (hidden, weight_grad.astype(jnp.bfloat16))


def solution(mesh):
    return jax.shard_map(
        local,
        mesh=mesh,
        in_specs=(P(("dp", "depth"), "grid"), P("grid", "depth"), P(("dp", "grid"), "depth")),
        out_specs=(P(("dp", "grid"), "depth"), P(("grid", "dp"), "depth")),
        check_vma=False,
    )
```

profile of v0, /device:TPU:0, one launch (start us, length us, event | category | flops | bytes accessed | tf_op | source)
XLA Modules:
  0.0 322.6 jit_solution(14169711380635420403)
XLA Ops:
  7.2 0.0 all-gather.3.cloned.1.call-start
  7.2 0.7 all-gather.3.cloned.1.call-update
  7.9 0.0 reduce-scatter.2.cloned.1.call-start
  7.9 157.1 %all-gather.3.cloned.1.call-done = bf16[1024,6144]{1,0:T(8,128)(2,1)} async-done(((bf16[64,6144]{1,0:T(8,128)(2,1)}), bf16[1024,6144]{1,0:T(8,128)(2,1)}) %all-gather.3.cloned.1.call-update) | async-done | bytes 12582928 | tf_op jit(solution)/shard_map/all_gather | solution.py:18
  165.0 31.6 %fusion.11 = f32[256,6144]{1,0:T(8,128)} fusion(bf16[6144,6144]{1,0:T(8,128)(2,1)} %param.4, bf16[1024,6144]{1,0:T(8,128)(2,1)} %all-gather.3.cloned.1.call-done, s32[]{:T(128)S(6)} %select_n.6), kind=kOutput, calls=%fused_computation.17 | convolution fusion | flops 19327352832 | bytes 84934656 | tf_op jit(solution)/shard_map/dot_general | solution.py:21
  196.6 0.0 copy-start
  196.6 0.0 reduce-scatter.2.cloned.1.call-update
  196.6 0.0 all-gather.5.cloned.1.call-start
  196.7 12.3 %reduce-scatter.2.cloned.1.call-done = f32[128,6144]{1,0:T(8,128)} async-done(((f32[256,6144]{1,0:T(8,128)}), f32[128,6144]{1,0:T(8,128)}) %reduce-scatter.2.cloned.1.call-update) | async-done | bytes 3145744 | tf_op jit(solution)/shard_map/reduce_scatter | solution.py:22
  209.0 0.0 copy-done
  209.0 4.9 %fusion.2 = (bf16[128,6144]{1,0:T(8,128)(2,1)}, bf16[128,6144]{1,0:T(8,128)(2,1)}) fusion(bf16[128,6144]{1,0:T(8,128)(2,1)S(1)} %copy-done, f32[128,6144]{1,0:T(8,128)} %reduce-scatter.2.cloned.1.call-done), kind=kLoop, calls=%fused_computation.7 | loop fusion | flops 18087936 | bytes 7864320 | tf_op jit(solution)/shard_map/convert_element_type | solution.py:25
  213.9 0.0 all-gather.5.cloned.1.call-update
  214.0 74.2 %all-gather.5.cloned.1.call-done = bf16[1024,6144]{1,0:T(8,128)(2,1)} async-done(((bf16[128,6144]{1,0:T(8,128)(2,1)}), bf16[1024,6144]{1,0:T(8,128)(2,1)}) %all-gather.5.cloned.1.call-update) | async-done | bytes 12582928 | tf_op jit(solution)/shard_map/all_gather | solution.py:29
  288.1 27.9 %convolution_convert_fusion = bf16[1536,6144]{1,0:T(8,128)(2,1)} fusion(bf16[1024,6144]{1,0:T(8,128)(2,1)} %all-gather.5.cloned.1.call-done, bf16[1024,6144]{1,0:T(8,128)(2,1)} %all-gather.3.cloned.1.call-done, s32[]{:T(128)S(6)} %select_n.7), kind=kOutput, calls=%fused_computation | convolution fusion | flops 19336790016 | bytes 34603012 | tf_op jit(solution)/shard_map/dot_general | solution.py:12
Async XLA Ops:
  7.2 157.8 %all-gather.3.cloned.1.call-start = ((), (), s32[]{:S(2)}) async-start(), calls=%async_computation.1 | async-start | bytes 13369344 | tf_op jit(solution)/shard_map/all_gather | solution.py:18
  7.9 201.1 %reduce-scatter.2.cloned.1.call-start = ((), (), s32[]{:S(2)}) async-start(), calls=%async_computation.2 | async-start | bytes 9437184 | tf_op jit(solution)/shard_map/reduce_scatter | solution.py:22
  196.6 12.4 %copy-start = (bf16[128,6144]{1,0:T(8,128)(2,1)S(1)}, bf16[128,6144]{1,0:T(8,128)(2,1)}, u32[]{:S(2)}) copy-start(bf16[128,6144]{1,0:T(8,128)(2,1)} %param.5) | copy-start | bytes 4718596
  196.6 91.5 %all-gather.5.cloned.1.call-start = ((), (), s32[]{:S(2)}) async-start(), calls=%async_computation.3 | async-start | bytes 14155776 | tf_op jit(solution)/shard_map/all_gather | solution.py:29
Sparse Core Ops, SparseCore 0:
  10.8 154.1 all-gather.2
  196.8 12.2 reduce-scatter.1
  214.1 73.9 all-gather.4
where the time goes:
time: 323 us
  waiting for transfers between devices  244 us (76%)
  matrix products  59.5 us (18%)
  between operations  13.8 us (4%)
  other arithmetic  4.9 us (2%)
    all_gather x1, waiting for transfers between devices, local(): all_rows = lax.all_gather(tokens, ('dp', 'depth'), axis=0, tiled=True)  157 us
    all_gather x1, waiting for transfers between devices, local(): lax.all_gather(grad_pre, ('dp', 'grid'), axis=0, tiled=True)  74.2 us
    dot_general x1, matrix products, local(): partial_pre = jnp.dot(own_rows, weight, preferred_element_type=jnp.float32)  31.6 us
    dot_general x1, matrix products, transposed_product(): lax.dot_general(left, right, (((0,), (0,)), ((), ())), preferred_element_...  27.9 us
    reduce_scatter x1, waiting for transfers between devices, local(): lax.psum_scatter(partial_pre, 'grid', scatter_dimension=0, tiled=True)  12.3 us
  transfers between devices with their start and end apart: 3, of which 3 were waited for; matrix products, arithmetic and copies ran while one was open for 0% of the time, Pallas kernels for 0%

commit v1 on v0

--- a/solution.py
+++ b/solution.py
@@ -15,7 +15,18 @@
 
 
 def local(tokens, weight, cotangent):
-    all_rows = lax.all_gather(tokens, ("dp", "depth"), axis=0, tiled=True)
+    top = lax.axis_size(("dp", "depth"))
+    a_next = lax.axis_index(("dp", "depth"))
+    known, piece_next = (top, a_next)
+    all_rows, block_out = (tokens, 1)
+    while block_out < known:
+        now = lax.ppermute(
+            all_rows, axis_name=("dp", "depth"), perm=[(j, j ^ block_out) for j in range(known)]
+        )
+        n_now = jnp.concatenate([all_rows, now], 0)
+        shaped = jnp.concatenate([now, all_rows], 0)
+        all_rows = jnp.where(piece_next & block_out == 0, n_now, shaped)
+        block_out = 2 * block_out
     group_size = all_rows.shape[0] // lax.axis_size("dp")
     own_rows = lax.dynamic_slice_in_dim(all_rows, lax.axis_index("dp") * group_size, group_size, 0)
     partial_pre = jnp.dot(own_rows, weight, preferred_element_type=jnp.float32)

time: 323 us -> 495 us (1.53)
  waiting for transfers between devices: 244 us -> 379 us
  other arithmetic: 4.9 us -> 33.5 us
  starting transfers between devices: 0.12 us -> 8.93 us
    ppermute x0 -> x4, waiting for transfers between devices: none -> 288 us  [local(): lax.ppermute(all_rows, axis_name=('dp', 'depth'), perm=[(j, j ^ block_out...]
    all_gather x1 -> x0, waiting for transfers between devices: 157 us -> none  [local(): all_rows = lax.all_gather(tokens, ('dp', 'depth'), axis=0, tiled=True)]
    select_n x0 -> x4, other arithmetic: none -> 28.6 us  [local(): all_rows = jnp.where(piece_next & block_out == 0, n_now, shaped)]
    ppermute x0 -> x4, starting transfers between devices: none -> 8.67 us  [local(): lax.ppermute(all_rows, axis_name=('dp', 'depth'), perm=[(j, j ^ block_out...]
  transfers between devices with their start and end apart: 3 -> 6, of which waited for: 3 -> 6; matrix products, arithmetic and copies ran while one was open for 0% -> 0% of each run, Pallas kernels for 0% -> 0%
where the time goes in v1:
time: 495 us
  waiting for transfers between devices  379 us (77%)
  matrix products  59.5 us (12%)
  other arithmetic  33.5 us (7%)
  between operations  14.1 us (3%)
  starting transfers between devices  8.93 us (2%)
    ppermute x4, waiting for transfers between devices, local(): lax.ppermute(all_rows, axis_name=('dp', 'depth'), perm=[(j, j ^ block_out...  288 us
    all_gather x1, waiting for transfers between devices, local(): lax.all_gather(grad_pre, ('dp', 'grid'), axis=0, tiled=True)  74.2 us
    dot_general x1, matrix products, local(): partial_pre = jnp.dot(own_rows, weight, preferred_element_type=jnp.float32)  31.6 us
    select_n x4, other arithmetic, local(): all_rows = jnp.where(piece_next & block_out == 0, n_now, shaped)  28.6 us
    dot_general x1, matrix products, transposed_product(): lax.dot_general(left, right, (((0,), (0,)), ((), ())), preferred_element_...  27.9 us
    reduce_scatter x1, waiting for transfers between devices, local(): lax.psum_scatter(partial_pre, 'grid', scatter_dimension=0, tiled=True)  16.8 us
  transfers between devices with their start and end apart: 6, of which 6 were waited for; matrix products, arithmetic and copies ran while one was open for 0% of the time, Pallas kernels for 0%

profile of v1, /device:TPU:0, one launch (start us, length us, event | category | flops | bytes accessed | tf_op | source)
XLA Modules:
  0.0 494.9 jit_solution(11295684810354950888)
XLA Ops:
  7.2 0.0 reduce-scatter.2.cloned.1.call-start
  7.2 3.1 collective-permute-start
  10.3 17.8 %collective-permute-done = bf16[64,6144]{1,0:T(8,128)(2,1)S(1)} collective-permute-done((bf16[64,6144]{1,0:T(8,128)(2,1)}, bf16[64,6144]{1,0:T(8,128)(2,1)S(1)}, u32[]{:S(2)}, u32[]{:S(2)}) %collective-permute-start) | collective-permute-done | bytes 786464 | tf_op jit(solution)/shard_map/ppermute | solution.py:23
  28.1 1.7 maximum_select_fusion.3
  29.8 0.0 copy-start
  29.8 2.8 collective-permute-start.1
  32.7 0.0 copy-done
  32.7 67.5 %collective-permute-done.1 = bf16[128,6144]{1,0:T(8,128)(2,1)} collective-permute-done((bf16[128,6144]{1,0:T(8,128)(2,1)S(1)}, bf16[128,6144]{1,0:T(8,128)(2,1)}, u32[]{:S(2)}, u32[]{:S(2)}) %collective-permute-start.1) | collective-permute-done | bytes 1572896 | tf_op jit(solution)/shard_map/ppermute | solution.py:23
  100.2 3.4 maximum_select_fusion.2
  103.6 1.4 collective-permute-start.2
  105.1 67.9 %collective-permute-done.2 = bf16[256,6144]{1,0:T(8,128)(2,1)} collective-permute-done((bf16[256,6144]{1,0:T(8,128)(2,1)S(1)}, bf16[256,6144]{1,0:T(8,128)(2,1)}, u32[]{:S(2)}, u32[]{:S(2)}) %collective-permute-start.2) | collective-permute-done | bytes 3145760 | tf_op jit(solution)/shard_map/ppermute | solution.py:23
  172.9 7.7 %maximum_select_fusion.1 = bf16[512,6144]{1,0:T(8,128)(2,1)} fusion(bf16[256,6144]{1,0:T(8,128)(2,1)} %collective-permute-done.2, bf16[256,6144]{1,0:T(8,128)(2,1)S(1)} %maximum_select_fusion.2, pred[]{:T(512)S(6)} %eq.13), kind=kLoop, calls=%fused_computation.2 | loop fusion | flops 28311552 | bytes 12582913 | tf_op jit(solution)/shard_map/jit(_where)/select_n | solution.py:28
  180.6 1.3 collective-permute-start.3
  181.9 134.7 %collective-permute-done.3 = bf16[512,6144]{1,0:T(8,128)(2,1)} collective-permute-done((bf16[512,6144]{1,0:T(8,128)(2,1)}, bf16[512,6144]{1,0:T(8,128)(2,1)}, u32[]{:S(2)}, u32[]{:S(2)}) %collective-permute-start.3) | collective-permute-done | bytes 6291488 | tf_op jit(solution)/shard_map/ppermute | solution.py:23
  316.6 15.8 %maximum_select_fusion = bf16[1024,6144]{1,0:T(8,128)(2,1)} fusion(bf16[512,6144]{1,0:T(8,128)(2,1)} %collective-permute-done.3, bf16[512,6144]{1,0:T(8,128)(2,1)} %maximum_select_fusion.1, pred[]{:T(512)S(6)} %eq.12), kind=kLoop, calls=%fused_computation.1 | loop fusion | flops 56623104 | bytes 25165824 | tf_op jit(solution)/shard_map/jit(_where)/select_n | solution.py:28
  332.3 31.6 %fusion.11 = f32[256,6144]{1,0:T(8,128)} fusion(bf16[6144,6144]{1,0:T(8,128)(2,1)} %param.4, bf16[1024,6144]{1,0:T(8,128)(2,1)} %maximum_select_fusion, s32[]{:T(128)S(6)} %select_n.46), kind=kOutput, calls=%fused_computation.20 | convolution fusion | flops 19327352832 | bytes 84934656 | tf_op jit(solution)/shard_map/dot_general | solution.py:32
  363.9 0.0 copy-start.1
  364.0 0.0 reduce-scatter.2.cloned.1.call-update
  364.0 0.2 all-gather.2.cloned.1.call-start
  364.2 16.8 %reduce-scatter.2.cloned.1.call-done = f32[128,6144]{1,0:T(8,128)} async-done(((f32[256,6144]{1,0:T(8,128)}), f32[128,6144]{1,0:T(8,128)}) %reduce-scatter.2.cloned.1.call-update) | async-done | bytes 3145744 | tf_op jit(solution)/shard_map/reduce_scatter | solution.py:33
  381.0 0.0 copy-done.1
  381.0 4.9 fusion.2
  385.9 0.0 all-gather.2.cloned.1.call-update
  385.9 74.2 %all-gather.2.cloned.1.call-done = bf16[1024,6144]{1,0:T(8,128)(2,1)} async-done(((bf16[128,6144]{1,0:T(8,128)(2,1)}), bf16[1024,6144]{1,0:T(8,128)(2,1)}) %all-gather.2.cloned.1.call-update) | async-done | bytes 12582928 | tf_op jit(solution)/shard_map/all_gather | solution.py:40
  460.1 27.9 %convolution_convert_fusion = bf16[1536,6144]{1,0:T(8,128)(2,1)} fusion(bf16[1024,6144]{1,0:T(8,128)(2,1)} %all-gather.2.cloned.1.call-done, bf16[1024,6144]{1,0:T(8,128)(2,1)} %maximum_select_fusion, s32[]{:T(128)S(6)} %select_n.47), kind=kOutput, calls=%fused_computation | convolution fusion | flops 19336790016 | bytes 34603012 | tf_op jit(solution)/shard_map/dot_general | solution.py:12
Async XLA Ops:
  7.2 373.8 %reduce-scatter.2.cloned.1.call-start = ((), (), s32[]{:S(2)}) async-start(), calls=%async_computation.1 | async-start | bytes 9437184 | tf_op jit(solution)/shard_map/reduce_scatter | solution.py:33
  7.2 20.9 %collective-permute-start = (bf16[64,6144]{1,0:T(8,128)(2,1)}, bf16[64,6144]{1,0:T(8,128)(2,1)S(1)}, u32[]{:S(2)}, u32[]{:S(2)}) collective-permute-start(bf16[64,6144]{1,0:T(8,128)(2,1)} %param.3), channel_id=1, source_target_pairs={{0,2},{2,0},{4,6},{6,4},{8,10},{10,8},{12,14},{14,12},{16,18},{18,... | collective-permute-start | bytes 2359304 | tf_op jit(solution)/shard_map/ppermute | solution.py:23
  29.8 2.8 copy-start
  29.8 70.3 %collective-permute-start.1 = (bf16[128,6144]{1,0:T(8,128)(2,1)S(1)}, bf16[128,6144]{1,0:T(8,128)(2,1)}, u32[]{:S(2)}, u32[]{:S(2)}) collective-permute-start(bf16[128,6144]{1,0:T(8,128)(2,1)S(1)} %maximum_select_fusion.3), channel_id=1, source_target_pairs={{0,4},{2,6},{4,0},{6,2},{8,12},{10,14},{12,8},{14,10},{16,20},{18,... | collective-permute-start | bytes 4718600 | tf_op jit(solution)/shard_map/ppermute | solution.py:23
  103.6 69.3 %collective-permute-start.2 = (bf16[256,6144]{1,0:T(8,128)(2,1)S(1)}, bf16[256,6144]{1,0:T(8,128)(2,1)}, u32[]{:S(2)}, u32[]{:S(2)}) collective-permute-start(bf16[256,6144]{1,0:T(8,128)(2,1)S(1)} %maximum_select_fusion.2), channel_id=1, source_target_pairs={{0,8},{2,10},{4,12},{6,14},{8,0},{10,2},{12,4},{14,6},{16,24},{18,... | collective-permute-start | bytes 9437192 | tf_op jit(solution)/shard_map/ppermute | solution.py:23
  180.6 136.0 %collective-permute-start.3 = (bf16[512,6144]{1,0:T(8,128)(2,1)}, bf16[512,6144]{1,0:T(8,128)(2,1)}, u32[]{:S(2)}, u32[]{:S(2)}) collective-permute-start(bf16[512,6144]{1,0:T(8,128)(2,1)} %maximum_select_fusion.1), channel_id=1, source_target_pairs={{0,16},{2,18},{4,20},{6,22},{8,24},{10,26},{12,28},{14,30},{16,0},... | collective-permute-start | bytes 18874376 | tf_op jit(solution)/shard_map/ppermute | solution.py:23
  363.9 17.0 %copy-start.1 = (bf16[128,6144]{1,0:T(8,128)(2,1)S(1)}, bf16[128,6144]{1,0:T(8,128)(2,1)}, u32[]{:S(2)}) copy-start(bf16[128,6144]{1,0:T(8,128)(2,1)} %param.5) | copy-start | bytes 4718596
  364.0 96.1 %all-gather.2.cloned.1.call-start = ((), (), s32[]{:S(2)}) async-start(), calls=%async_computation.2 | async-start | bytes 14155776 | tf_op jit(solution)/shard_map/all_gather | solution.py:40
Sparse Core Ops, SparseCore 0:
  364.1 16.8 reduce-scatter.1
  386.0 74.0 all-gather.1
